TPU v7x, 512 devices: a whole 4x4x16 slice. The times are simulated.
512 devices in a mesh: tile: 64 (over z, y), lev: 8 (over x, core).
Axes of the slice: x: 4, y: 4, z: 16, core: 2. Of those that a mesh axis runs over, the one named last changes fastest.
Arguments:
- store: float32 [8, 4096, 8, 4, 128], P('lev', 'tile'), may hold values from -6 to 6
- placement: int32 [32, 4096], P('lev', 'tile'), may hold values from 0 to 511, as said below
- wet: int32 [4096, 128], P('tile'), may hold values 0 or 1
- kappa: float32 [32], P('lev'), may hold values from 0.1 to 1
- thickness: float32 [32], P('lev'), may hold values from 0.5 to 2
- cotangent: float32 [4, 32, 4096, 128], P(None, 'lev', 'tile'), may hold values from -6 to 6
Outputs:
- adjoint_state: float32 [4, 32, 4096, 128], P(None, 'lev', 'tile')
Inputs may be any that keep to these rules, and one draw needn't show every extreme that they name: `placement`: within the 4 x 64 entries of one device the values are distinct; value v names slot v % 8 of holder tile v // 8 on the same level slab; in each device's block of 4 x 64 entries at least one holder tile supplies all 8 of its slots.
All inputs are finite; a program needn't handle non-finite values. No bound on the sum of `wet` on one device may be relied on, other than what follows from the above.
Results may differ from a plain program's by a relative error of at most 0.00002.
Values sent between devices are 32-bit elements; how exact they have to be, the bound alone decides.
A program may use at most 64 MiB of HBM per device.

v0:
```python
import jax
import jax.numpy as jnp
from jax import lax
from jax.sharding import PartitionSpec as P


def carried_in(x, axis, combine, identity, reverse):
    size, position = (lax.axis_size(axis), lax.axis_index(axis))
    everything = lax.all_gather(x, axis)
    start = jnp.broadcast_to(jnp.asarray(identity, x.dtype), x.shape)

    def step(k, before):
        at = size - 1 - k if reverse else k
        reached = at > position if reverse else at < position
        new = combine(before, everything[at])
        return jnp.where(reached, new, before)

    return lax.fori_loop(0, size, step, start)


def with_halo(x, sides, width):
    for axis, dim in sides:
        size, length = (lax.axis_size(axis), x.shape[dim])
        up = [(i, (i + 1) % size) for i in range(size)]
        down = [(j, i) for i, j in up]
        last = lax.slice_in_dim(x, length - width, length, axis=dim)
        initial = lax.slice_in_dim(x, 0, width, axis=dim)
        before = lax.ppermute(last, axis, up)
        after = lax.ppermute(initial, axis, down)
        x = jnp.concatenate([before, x, after], axis=dim)
    return x


def passed_along(block, axis, distance):
    devices = range(lax.axis_size(axis))
    route = [((i - distance) % len(devices), i) for i in devices]
    return lax.ppermute(block, axis, route)


def plus(earlier, later):
    return earlier + later


def lower_total(slab):
    return carried_in(slab, "lev", plus, jnp.zeros_like(slab), False)


def upper_total(slab):
    return carried_in(slab, "lev", plus, jnp.zeros_like(slab), True)


def recompute(state, thickness):
    warmth, salinity = (state[0], state[1])
    density = -0.25 * warmth + 0.75 * salinity - 0.05 * warmth * warmth
    layered = density * thickness[:, None, None]
    below = lower_total(jnp.sum(layered, axis=0))
    pressure = 0.2 * (below[None] + jnp.cumsum(layered, axis=0) - 0.5 * layered)
    return with_halo(jnp.stack([pressure, warmth, salinity]), (("tile", 2),), 1)


def slope_x(padded):
    return (padded[:, 2:] - padded[:, :-2]) * 0.5


def slope_y(center):
    return (jnp.roll(center, -1, 2) - jnp.roll(center, 1, 2)) * 0.5


def laplace(padded):
    center = padded[:, 1:-1]
    return (
        padded[:, 2:]
        + padded[:, :-2]
        + jnp.roll(center, -1, 2)
        + jnp.roll(center, 1, 2)
        - 4.0 * center
    )


def advance(padded, zonal, meridional, ocean, diffuse):
    pressure_pad, warm_pad, salt_pad = (padded[0], padded[1], padded[2])
    pressure = pressure_pad[:, 1:-1]
    warmth = warm_pad[:, 1:-1]
    salinity = salt_pad[:, 1:-1]
    zonal_new = zonal + 0.2 * ocean * (-slope_x(pressure_pad) + 0.5 * meridional)
    merid_new = meridional + 0.2 * ocean * (-slope_y(pressure) - 0.5 * zonal)
    warm_new = warmth + 0.2 * ocean * (
        diffuse * laplace(warm_pad) - zonal * slope_x(warm_pad) - meridional * slope_y(warmth)
    )
    salt_new = salinity + 0.2 * ocean * (
        diffuse * laplace(salt_pad) - zonal * slope_x(salt_pad) - meridional * slope_y(salinity)
    )
    return jnp.stack([warm_new, salt_new, zonal_new, merid_new])


def backward(adjoint_new, padded, zonal, meridional, ocean, diffuse, thickness):

    def local_step(padded_in, zonal_in, merid_in):
        return advance(padded_in, zonal_in, merid_in, ocean, diffuse)

    _, pullback = jax.vjp(local_step, padded, zonal, meridional)
    adjoint_pad, adjoint_zonal, adjoint_merid = pullback(adjoint_new)
    low_rim = adjoint_pad[:, :, 0, :]
    high_rim = adjoint_pad[:, :, -1, :]
    from_right = passed_along(low_rim, "tile", -1)
    from_left = passed_along(high_rim, "tile", 1)
    core = adjoint_pad[:, :, 1:-1, :]
    core = core.at[:, :, -1, :].add(from_right)
    core = core.at[:, :, 0, :].add(from_left)
    adjoint_pressure, adjoint_warm, adjoint_salt = (core[0], core[1], core[2])
    adjoint_below = 0.2 * jnp.sum(adjoint_pressure, axis=0)
    adjoint_layered = 0.2 * (
        lax.cumsum(adjoint_pressure, axis=0, reverse=True) - 0.5 * adjoint_pressure
    )
    adjoint_layered = adjoint_layered + upper_total(adjoint_below)[None]
    adjoint_density = adjoint_layered * thickness[:, None, None]
    warmth = padded[1][:, 1:-1]
    adjoint_warm = adjoint_warm + adjoint_density * (-0.25 - 0.1 * warmth)
    adjoint_salt = adjoint_salt + 0.75 * adjoint_density
    return jnp.stack([adjoint_warm, adjoint_salt, adjoint_zonal, adjoint_merid])


def per_device(store, placement, wet, kappa, thickness, cotangent):
    held = store[0]
    levels, rows = placement.shape
    width = held.shape[-1]
    wanted = placement.reshape(-1)
    arrived = lax.all_to_all(held, "tile", split_axis=0, concat_axis=0, tiled=True)
    flat_slots = arrived.reshape(-1, 4, width)
    pieces = jnp.take(flat_slots, wanted, axis=0)
    start_state = jnp.transpose(pieces.reshape(levels, rows, 4, width), (2, 0, 1, 3))
    ocean = wet.astype(jnp.float32)[None]
    diffuse = kappa[:, None, None]
    padded_first = recompute(start_state, thickness)
    middle_state = advance(padded_first, start_state[2], start_state[3], ocean, diffuse)
    padded_second = recompute(middle_state, thickness)
    adjoint_middle = backward(
        cotangent, padded_second, middle_state[2], middle_state[3], ocean, diffuse, thickness
    )
    return backward(
        adjoint_middle, padded_first, start_state[2], start_state[3], ocean, diffuse, thickness
    )


def solution(mesh):
    placed = (
        P("lev", "tile", None, None, None),
        P("lev", "tile"),
        P("tile", None),
        P("lev"),
        P("lev"),
        P(None, "lev", "tile", None),
    )
    return jax.shard_map(
        per_device,
        mesh=mesh,
        in_specs=placed,
        out_specs=P(None, "lev", "tile", None),
        check_vma=False,
    )
```

profile of v0, /device:TPU:1, one launch (start us, length us, event | category | flops | bytes accessed | tf_op | source)
XLA Modules:
  0.0 196.9 jit_solution(7476466956041435553)
XLA Ops:
  0.0 19.3 %all-to-all-start = ((f32[64,8,4,128]{3,2,1,0:T(4,128)}), f32[64,8,4,128]{3,2,1,0:T(4,128)S(1)}, u32[]{:S(2)}, u32[]{:S(2)}) async-start(f32[64,8,4,128]{3,2,1,0:T(4,128)} %bitcast.265), calls=%async_computation | async-start | bytes 2097152 | tf_op jit(solution)/shard_map/all_to_all | solution.py:128
  19.3 0.7 copy-done.16
  20.1 50.6 %all-to-all-done = f32[64,8,4,128]{3,2,1,0:T(4,128)S(1)} async-done(((f32[64,8,4,128]{3,2,1,0:T(4,128)}), f32[64,8,4,128]{3,2,1,0:T(4,128)S(1)}, u32[]{:S(2)}, u32[]{:S(2)}) %all-to-all-start) | async-done | bytes 1048608 | tf_op jit(solution)/shard_map/all_to_all | solution.py:128
  70.7 1.0 gather_fusion
  71.7 0.1 fusion.5
  71.9 0.6 copy-done.12
  72.6 17.8 %all-gather = f32[512,128]{1,0:T(8,128)S(1)} all-gather(f32[64,128]{1,0:T(8,128)S(1)} %fusion.9), channel_id=2, replica_groups=mesh['tile'=64,'lev'=8] {'lev'}, dimensions={0}, use_global_device_ids=true | all-gather | bytes 294912 | tf_op jit(solution)/shard_map/all_gather | solution.py:9
  90.4 0.3 while.64
  90.7 0.1 fusion.3
  90.9 3.1 %collective-permute-start = (f32[3,4,1,128]{3,2,1,0:T(1,128)S(1)}, f32[3,4,1,128]{3,2,1,0:T(1,128)S(1)}, u32[]{:S(2)}, u32[]{:S(2)}) collective-permute-start(f32[3,4,1,128]{3,2,1,0:T(1,128)S(1)} %get-tuple-element.600), channel_id=1, source_target_pairs={{0,8},{8,16},{16,24},{24,32},{32,40},{40,48},{48,56},{56,64},{64,7... | collective-permute-start | bytes 18440 | tf_op jit(solution)/shard_map/ppermute | solution.py:28
  94.0 5.5 %collective-permute-start.1 = (f32[3,4,1,128]{3,2,1,0:T(1,128)S(1)}, f32[3,4,1,128]{3,2,1,0:T(1,128)S(1)}, u32[]{:S(2)}, u32[]{:S(2)}) collective-permute-start(f32[3,4,1,128]{3,2,1,0:T(1,128)S(1)} %get-tuple-element.601), channel_id=1, source_target_pairs={{8,0},{16,8},{24,16},{32,24},{40,32},{48,40},{56,48},{64,56},{72,6... | collective-permute-start | bytes 18440 | tf_op jit(solution)/shard_map/ppermute | solution.py:29
  99.5 0.7 collective-permute-done.1
  100.3 0.1 fusion.103
  100.5 0.1 fusion.102
  100.6 0.1 fusion.96
  100.7 0.1 fusion.97
  100.8 0.6 copy-done.17
  101.5 0.3 fusion.78
  101.8 14.0 %all-gather.2 = f32[512,128]{1,0:T(8,128)S(1)} all-gather(f32[64,128]{1,0:T(8,128)S(1)} %get-tuple-element.556), channel_id=4, replica_groups=mesh['tile'=64,'lev'=8] {'lev'}, dimensions={0}, use_global_device_ids=true | all-gather | bytes 294912 | tf_op jit(solution)/shard_map/all_gather | solution.py:9
  115.8 0.3 while.66
  116.1 0.6 copy-done.13
  116.7 0.1 fusion.4
  116.9 2.1 %collective-permute-start.4 = (f32[3,4,1,128]{3,2,1,0:T(1,128)S(1)}, f32[3,4,1,128]{3,2,1,0:T(1,128)S(1)}, u32[]{:S(2)}, u32[]{:S(2)}) collective-permute-start(f32[3,4,1,128]{3,2,1,0:T(1,128)S(1)} %get-tuple-element.598), channel_id=1, source_target_pairs={{0,8},{8,16},{16,24},{24,32},{32,40},{40,48},{48,56},{56,64},{64,7... | collective-permute-start | bytes 18440 | tf_op jit(solution)/shard_map/ppermute | solution.py:28
  118.9 7.2 %collective-permute-start.5 = (f32[3,4,1,128]{3,2,1,0:T(1,128)S(1)}, f32[3,4,1,128]{3,2,1,0:T(1,128)S(1)}, u32[]{:S(2)}, u32[]{:S(2)}) collective-permute-start(f32[3,4,1,128]{3,2,1,0:T(1,128)S(1)} %get-tuple-element.599), channel_id=1, source_target_pairs={{8,0},{16,8},{24,16},{32,24},{40,32},{48,40},{56,48},{64,56},{72,6... | collective-permute-start | bytes 18440 | tf_op jit(solution)/shard_map/ppermute | solution.py:29
  126.2 0.2 fusion.89
  126.5 0.4 collective-permute-done.5
  127.0 0.6 copy-done.18
  127.6 0.9 fusion.61
  129.0 0.8 fusion.98
  129.8 0.8 fusion.99
  130.6 0.8 fusion.100
  131.3 0.8 fusion.101
  132.4 0.1 add_add_fusion.5
  132.6 0.1 add_add_fusion.7
  132.7 0.2 fusion.57
  133.0 0.1 add_add_fusion.6
  133.3 6.9 %collective-permute-start.2 = (f32[3,4,128]{2,1,0:T(4,128)S(1)}, f32[3,4,128]{2,1,0:T(4,128)S(1)}, u32[]{:S(2)}, u32[]{:S(2)}) collective-permute-start(f32[3,4,128]{2,1,0:T(4,128)S(1)} %bitcast.276), channel_id=1, source_target_pairs={{8,0},{16,8},{24,16},{32,24},{40,32},{48,40},{56,48},{64,56},{72,6... | collective-permute-start | bytes 18440 | tf_op jit(solution)/shard_map/ppermute | solution.py:37
  140.3 0.3 copy.40
  140.6 1.9 collective-permute-start.3
  142.5 5.7 %collective-permute-done.3 = f32[3,4,128]{2,1,0:T(4,128)S(1)} collective-permute-done((f32[3,4,128]{2,1,0:T(4,128)S(1)}, f32[3,4,128]{2,1,0:T(4,128)S(1)}, u32[]{:S(2)}, u32[]{:S(2)}) %collective-permute-start.3) | collective-permute-done | bytes 6176 | tf_op jit(solution)/shard_map/ppermute | solution.py:37
  148.3 0.8 slice_bitcast_fusion.4
  149.1 15.4 %all-gather.1 = f32[512,128]{1,0:T(8,128)S(1)} all-gather(f32[64,128]{1,0:T(8,128)S(1)} %broadcast_multiply_fusion.1), channel_id=3, replica_groups=mesh['tile'=64,'lev'=8] {'lev'}, dimensions={0}, use_global_device_ids=true | all-gather | bytes 294912 | tf_op jit(solution)/shard_map/all_gather | solution.py:9
  164.5 0.3 while.65
  164.8 1.1 reduce_window_sum.36
  165.9 0.7 copy-done.14
  166.7 0.8 copy-done.1
  167.5 0.1 fusion.81
  167.6 0.7 copy-done.4
  168.8 0.3 fusion.80
  169.1 0.1 fusion.107
  170.1 0.1 add_add_fusion
  170.2 0.7 copy-done.2
  171.1 0.1 add_add_fusion.4
  171.2 0.1 add_add_fusion.3
  171.4 0.1 add_add_fusion.2
  171.6 0.1 add_add_fusion.1
  171.8 1.9 collective-permute-start.6
  173.8 3.4 %collective-permute-start.7 = (f32[3,4,128]{2,1,0:T(4,128)S(1)}, f32[3,4,128]{2,1,0:T(4,128)S(1)}, u32[]{:S(2)}, u32[]{:S(2)}) collective-permute-start(f32[3,4,128]{2,1,0:T(4,128)S(1)} %bitcast.273), channel_id=1, source_target_pairs={{504,0},{0,8},{8,16},{16,24},{24,32},{32,40},{40,48},{48,56},{56,6... | collective-permute-start | bytes 18440 | tf_op jit(solution)/shard_map/ppermute | solution.py:37
  177.1 0.3 add_bitcast_fusion.7
  177.5 0.3 copy.43
  177.8 3.6 %collective-permute-done.7 = f32[3,4,128]{2,1,0:T(4,128)S(1)} collective-permute-done((f32[3,4,128]{2,1,0:T(4,128)S(1)}, f32[3,4,128]{2,1,0:T(4,128)S(1)}, u32[]{:S(2)}, u32[]{:S(2)}) %collective-permute-start.7) | collective-permute-done | bytes 6176 | tf_op jit(solution)/shard_map/ppermute | solution.py:37
  181.5 14.0 %all-gather.3 = f32[512,128]{1,0:T(8,128)S(1)} all-gather(f32[64,128]{1,0:T(8,128)S(1)} %broadcast_multiply_fusion), channel_id=5, replica_groups=mesh['tile'=64,'lev'=8] {'lev'}, dimensions={0}, use_global_device_ids=true | all-gather | bytes 294912 | tf_op jit(solution)/shard_map/all_gather | solution.py:9
  195.5 0.3 while.67
  196.1 0.8 pad_maximum_fusion
  (127 shorter events, 3.9 us)
Async XLA Ops:
  0.0 70.7 %all-to-all-start = ((f32[64,8,4,128]{3,2,1,0:T(4,128)}), f32[64,8,4,128]{3,2,1,0:T(4,128)S(1)}, u32[]{:S(2)}, u32[]{:S(2)}) async-start(f32[64,8,4,128]{3,2,1,0:T(4,128)} %bitcast.265), calls=%async_computation | async-start | bytes 2097152 | tf_op jit(solution)/shard_map/all_to_all | solution.py:128
  19.3 0.7 copy-start.16
  71.9 0.7 copy-start.12
  90.8 8.7 %copy-start.15 = (s32[64,128]{1,0:T(8,128)S(1)}, s32[64,128]{1,0:T(8,128)}, u32[]{:S(2)}) copy-start(s32[64,128]{1,0:T(8,128)} %param.24) | copy-start | bytes 98308
  90.9 8.7 %collective-permute-start = (f32[3,4,1,128]{3,2,1,0:T(1,128)S(1)}, f32[3,4,1,128]{3,2,1,0:T(1,128)S(1)}, u32[]{:S(2)}, u32[]{:S(2)}) collective-permute-start(f32[3,4,1,128]{3,2,1,0:T(1,128)S(1)} %get-tuple-element.600), channel_id=1, source_target_pairs={{0,8},{8,16},{16,24},{24,32},{32,40},{40,48},{48,56},{56,64},{64,7... | collective-permute-start | bytes 18440 | tf_op jit(solution)/shard_map/ppermute | solution.py:28
  94.0 6.3 %collective-permute-start.1 = (f32[3,4,1,128]{3,2,1,0:T(1,128)S(1)}, f32[3,4,1,128]{3,2,1,0:T(1,128)S(1)}, u32[]{:S(2)}, u32[]{:S(2)}) collective-permute-start(f32[3,4,1,128]{3,2,1,0:T(1,128)S(1)} %get-tuple-element.601), channel_id=1, source_target_pairs={{8,0},{16,8},{24,16},{32,24},{40,32},{48,40},{56,48},{64,56},{72,6... | collective-permute-start | bytes 18440 | tf_op jit(solution)/shard_map/ppermute | solution.py:29
  100.8 0.7 copy-start.17
  116.1 0.7 copy-start.13
  116.7 9.4 %copy-start = (f32[4,4,64,128]{3,2,1,0:T(8,128)S(1)}, f32[4,4,64,128]{3,2,1,0:T(8,128)}, u32[]{:S(2)}) copy-start(f32[4,4,64,128]{3,2,1,0:T(8,128)} %param.27) | copy-start | bytes 1572868
  116.9 9.7 %collective-permute-start.4 = (f32[3,4,1,128]{3,2,1,0:T(1,128)S(1)}, f32[3,4,1,128]{3,2,1,0:T(1,128)S(1)}, u32[]{:S(2)}, u32[]{:S(2)}) collective-permute-start(f32[3,4,1,128]{3,2,1,0:T(1,128)S(1)} %get-tuple-element.598), channel_id=1, source_target_pairs={{0,8},{8,16},{16,24},{24,32},{32,40},{40,48},{48,56},{56,64},{64,7... | collective-permute-start | bytes 18440 | tf_op jit(solution)/shard_map/ppermute | solution.py:28
  118.9 8.0 %collective-permute-start.5 = (f32[3,4,1,128]{3,2,1,0:T(1,128)S(1)}, f32[3,4,1,128]{3,2,1,0:T(1,128)S(1)}, u32[]{:S(2)}, u32[]{:S(2)}) collective-permute-start(f32[3,4,1,128]{3,2,1,0:T(1,128)S(1)} %get-tuple-element.599), channel_id=1, source_target_pairs={{8,0},{16,8},{24,16},{32,24},{40,32},{48,40},{56,48},{64,56},{72,6... | collective-permute-start | bytes 18440 | tf_op jit(solution)/shard_map/ppermute | solution.py:29
  126.9 0.7 copy-start.18
  133.3 9.2 %collective-permute-start.2 = (f32[3,4,128]{2,1,0:T(4,128)S(1)}, f32[3,4,128]{2,1,0:T(4,128)S(1)}, u32[]{:S(2)}, u32[]{:S(2)}) collective-permute-start(f32[3,4,128]{2,1,0:T(4,128)S(1)} %bitcast.276), channel_id=1, source_target_pairs={{8,0},{16,8},{24,16},{32,24},{40,32},{48,40},{56,48},{64,56},{72,6... | collective-permute-start | bytes 18440 | tf_op jit(solution)/shard_map/ppermute | solution.py:37
  140.6 7.7 %collective-permute-start.3 = (f32[3,4,128]{2,1,0:T(4,128)S(1)}, f32[3,4,128]{2,1,0:T(4,128)S(1)}, u32[]{:S(2)}, u32[]{:S(2)}) collective-permute-start(f32[3,4,128]{2,1,0:T(4,128)S(1)} %bitcast.275), channel_id=1, source_target_pairs={{504,0},{0,8},{8,16},{16,24},{24,32},{32,40},{40,48},{48,56},{56,6... | collective-permute-start | bytes 18440 | tf_op jit(solution)/shard_map/ppermute | solution.py:37
  165.9 0.7 copy-start.14
  166.6 0.9 copy-start.1
  167.5 0.9 copy-start.4
  167.5 1.0 copy-start.5
  167.5 1.0 copy-start.6
  167.5 1.1 copy-start.7
  167.5 1.2 copy-start.8
  167.5 1.2 copy-start.9
  167.5 1.2 copy-start.10
  167.5 1.2 copy-start.11
  167.6 1.1 copy-start.19
  170.1 0.9 copy-start.2
  170.1 1.0 copy-start.3
  171.8 5.9 %collective-permute-start.6 = (f32[3,4,128]{2,1,0:T(4,128)S(1)}, f32[3,4,128]{2,1,0:T(4,128)S(1)}, u32[]{:S(2)}, u32[]{:S(2)}) collective-permute-start(f32[3,4,128]{2,1,0:T(4,128)S(1)} %bitcast.274), channel_id=1, source_target_pairs={{8,0},{16,8},{24,16},{32,24},{40,32},{48,40},{56,48},{64,56},{72,6... | collective-permute-start | bytes 18440 | tf_op jit(solution)/shard_map/ppermute | solution.py:37
  173.8 7.7 %collective-permute-start.7 = (f32[3,4,128]{2,1,0:T(4,128)S(1)}, f32[3,4,128]{2,1,0:T(4,128)S(1)}, u32[]{:S(2)}, u32[]{:S(2)}) collective-permute-start(f32[3,4,128]{2,1,0:T(4,128)S(1)} %bitcast.273), channel_id=1, source_target_pairs={{504,0},{0,8},{8,16},{16,24},{24,32},{32,40},{40,48},{48,56},{56,6... | collective-permute-start | bytes 18440 | tf_op jit(solution)/shard_map/ppermute | solution.py:37
where the time goes:
time: 198 us; the launch traced here: 197 us
  blocking collectives  61.2 us (31%)
  waiting for transfers between devices  61.1 us (31%)
  starting transfers between devices  51.3 us (26%)
  local copies, waits for them, and re-layouts  13.8 us (7%)
  other arithmetic  7.8 us (4%)
    all_gather x4, blocking collectives, carried_in(): everything = lax.all_gather(x, axis)  61.2 us
    all_to_all x1, waiting for transfers between devices, per_device(): lax.all_to_all(held, 'tile', split_axis=0, concat_axis=0, tiled=True)  50.6 us
    all_to_all x1, starting transfers between devices, per_device(): lax.all_to_all(held, 'tile', split_axis=0, concat_axis=0, tiled=True)  19.3 us
    ppermute x4, starting transfers between devices, passed_along(): return lax.ppermute(block, axis, route)  14.1 us
    ppermute x2, starting transfers between devices, with_halo(): after = lax.ppermute(initial, axis, down)  12.8 us
    ppermute x4, waiting for transfers between devices, passed_along(): return lax.ppermute(block, axis, route)  9.38 us
    unnamed x42, local copies, waits for them, and re-layouts  7.18 us
    ppermute x2, starting transfers between devices, with_halo(): before = lax.ppermute(last, axis, up)  5.13 us
  transfers between devices with their start and end apart: 9, of which 5 were waited for; matrix products, arithmetic and copies ran while one was open for 1% of the time, Pallas kernels for 0%

commit v1 on v0

v1 whole, which is shorter than its diff:
```python
import jax
import jax.numpy as jnp
from jax import lax
from jax.experimental import pallas as pl
from jax.experimental.pallas import tpu as pltpu
from jax.sharding import PartitionSpec as P

MESH = pl.DeviceIdType.MESH
LEVELS = 4
ROWS = 64
CELLS = 128
PAD = 72
EDGE = 4
SLOTS = 8
TILES = 64
RING = 16
SIDE = 4
SLABS = 8
HALO = 3
RIM = 2


def before(x):
    return pltpu.roll(x, 1, 0)


def after(x):
    return pltpu.roll(x, PAD - 1, 0)


def slope_x(x):
    return 0.5 * (after(x) - before(x))


def slope_y(x):
    return 0.5 * (pltpu.roll(x, CELLS - 1, 1) - pltpu.roll(x, 1, 1))


def stencil(x):
    down, up = after(x), before(x)
    right, left = pltpu.roll(x, CELLS - 1, 1), pltpu.roll(x, 1, 1)
    return 0.5 * (down - up), 0.5 * (right - left), (down + up) + (right + left) - 4.0 * x


def laplace(x):
    return stencil(x)[2]


def kernel(
    store, placement, wet, kappa, thickness, cotangent, out,
    slots, state, halo_out, halo_in, place, wet_in, scale, thick, cot, rim_out, rim_in,
    lam, mask, total, totals, both, boths,
    drive_p, mul_t, mul_s, base_t, base_s, base_u, base_v, bend,
    heat, layer, push_u, push_v, grad, later_t, later_s, adj_q, result,
    load_sem, ready_sem, slot_send, slot_recv, own_sem, halo_send, halo_recv,
    rim_send, rim_recv, total_send, total_recv, both_send, both_recv, out_sem,
):
    me = lax.axis_index("tile")
    lev = lax.axis_index("lev")
    z, y = me // SIDE, lax.rem(me, SIDE)

    def tile_at(dz, dy):
        return lax.rem(z + (dz + RING), RING) * SIDE + lax.rem(y + dy, SIDE)

    def signal(sem, **where):
        pl.semaphore_signal(sem, inc=1, device_id=where, device_id_type=MESH)

    greet = pltpu.get_barrier_semaphore()
    for dz in (1, -1, 2, -2):
        signal(greet, tile=tile_at(dz, 0))
    for dy in (1, 2, 3):
        signal(greet, tile=tile_at(0, dy))
    for k in range(1, SLABS):
        signal(greet, lev=lax.rem(lev + k, SLABS))

    loads = [
        pltpu.make_async_copy(cotangent, cot, load_sem.at[0]),
        pltpu.make_async_copy(wet, wet_in, load_sem.at[1]),
        pltpu.make_async_copy(placement, place, load_sem.at[2]),
        pltpu.make_async_copy(kappa, scale, load_sem.at[3]),
        pltpu.make_async_copy(thickness, thick, load_sem.at[4]),
    ]
    for load in loads:
        load.start()
    own = pltpu.make_async_copy(
        store.at[pl.ds(me * SLOTS, SLOTS)], slots.at[pl.ds(me * SLOTS, SLOTS)], own_sem
    )
    own.start()

    def send_slots(to):
        pltpu.make_async_remote_copy(
            src_ref=store.at[pl.ds(to * SLOTS, SLOTS)],
            dst_ref=slots.at[pl.ds(me * SLOTS, SLOTS)],
            send_sem=slot_send,
            recv_sem=slot_recv,
            device_id={"tile": to},
            device_id_type=MESH,
        ).start()

    def send_ring(first, last):
        @pl.loop(first * 8, last * 8)
        def _(i):
            reach = i // 8
            towards = 1 - 2 * lax.rem(i, 2)
            send_slots(tile_at(reach * towards, lax.rem(i // 2, SIDE)))

    for load in loads:
        load.wait()
    mask[EDGE : EDGE + ROWS] = 0.2 * wet_in[...].astype(jnp.float32)
    rim_out[0, 32:34] = 0.2 * wet_in[0:RIM].astype(jnp.float32)
    rim_out[1, 32:34] = 0.2 * wet_in[ROWS - RIM : ROWS].astype(jnp.float32)
    for f in range(4):
        for l in range(LEVELS):
            i = f * LEVELS + l
            lam[f, l, EDGE : EDGE + ROWS] = cot[f, l]
            rim_out[0, i * RIM : (i + 1) * RIM] = cot[f, l, 0:RIM]
            rim_out[1, i * RIM : (i + 1) * RIM] = cot[f, l, ROWS - RIM : ROWS]

    pl.semaphore_wait(greet, 7 + SLABS - 1)
    for dy in (1, 2, 3):
        signal(ready_sem.at[0], tile=tile_at(0, dy))
    for dy in (1, 2, 3):
        send_slots(tile_at(0, dy))
    pl.semaphore_wait(ready_sem.at[0], 3)
    for dz in (2, -2):
        signal(ready_sem.at[1], tile=tile_at(dz, 0))

    left, right = lax.rem(me + TILES - 1, TILES), lax.rem(me + 1, TILES)

    def to_neighbours(outgoing, incoming, send, recv):
        return [
            pltpu.make_async_remote_copy(
                src_ref=outgoing.at[side],
                dst_ref=incoming.at[side],
                send_sem=send.at[side],
                recv_sem=recv.at[side],
                device_id={"tile": to},
                device_id_type=MESH,
            )
            for side, to in ((0, left), (1, right))
        ]

    rims = to_neighbours(rim_out, rim_in, rim_send, rim_recv)
    for copy in rims:
        copy.start()
    send_ring(1, 3)
    pl.semaphore_wait(ready_sem.at[1], 2)
    for dz in (4, -4):
        signal(ready_sem.at[2], tile=tile_at(dz, 0))
    send_ring(3, 5)
    pl.semaphore_wait(ready_sem.at[2], 2)

    for copy in rims:
        copy.wait()
    for side, at in ((0, EDGE + ROWS), (1, EDGE - RIM)):
        mask[at : at + RIM] = rim_in[side, 32:34]
        for f in range(4):
            for l in range(LEVELS):
                i = f * LEVELS + l
                lam[f, l, at : at + RIM] = rim_in[side, i * RIM : (i + 1) * RIM]

    total[...] = jnp.zeros_like(total)

    @pl.loop(0, LEVELS)
    def _(l):
        m = mask[...]
        p = slope_x(m * lam[2, l]) + slope_y(m * lam[3, l])
        drive_p[l] = p
        total[...] += p

    def to_slabs(source, incoming, send, recv):
        for k in range(1, SLABS):
            to = lax.rem(lev + k, SLABS)
            pltpu.make_async_remote_copy(
                src_ref=source((lev + k) // SLABS),
                dst_ref=incoming.at[k - 1],
                send_sem=send,
                recv_sem=recv,
                device_id={"lev": to},
                device_id_type=MESH,
            ).start()

    def whole(ref, sem):
        pltpu.make_async_copy(ref, ref, sem).wait()

    to_slabs(lambda turn: total, totals, total_send, total_recv)

    for dy in range(SIDE):
        send_slots(tile_at(RING // 2, dy))

    @pl.loop(0, 24)
    def _(i):
        towards = 1 - 2 * lax.rem(i, 2)
        send_slots(tile_at((7 - i // 8) * towards, lax.rem(i // 2, SIDE)))

    whole(totals, total_recv)
    whole(totals, total_send)
    total_above = jnp.zeros((PAD, CELLS), jnp.float32)
    for k in range(1, SLABS):
        total_above += jnp.where(k > lev, totals[k - 1], 0.0)

    def second_step(j, running):
        l = LEVELS - 1 - j
        m = mask[...]
        p = drive_p[l]
        running = running + p
        density = 0.2 * (running - 0.5 * p) * thick[l]
        lt, ls, lu, lv = lam[0, l], lam[1, l], lam[2, l], lam[3, l]
        a, b = m * lt, m * ls
        mul_t[l] = a
        mul_s[l] = b
        base_t[l] = lt + scale[l] * laplace(a) - 0.25 * density
        base_s[l] = ls + scale[l] * laplace(b) + 0.75 * density
        base_u[l] = lu - 0.5 * (m * lv)
        base_v[l] = lv + 0.5 * (m * lu)
        bend[l] = 0.1 * density
        return running

    lax.fori_loop(0, LEVELS, second_step, total_above)

    own.wait()
    arrived = slots.at[pl.ds(0, (TILES - 1) * SLOTS)]
    whole(arrived, slot_recv)

    field = LEVELS * PAD
    for l in range(LEVELS):
        for r in range(HALO):
            halo_out[0, l * HALO + r] = slots[place[l, r]]
            halo_out[1, l * HALO + r] = slots[place[l, ROWS - HALO + r]]
    halos = to_neighbours(halo_out, halo_in, halo_send, halo_recv)
    for copy in halos:
        copy.start()

    for l in range(LEVELS):

        @pl.loop(0, ROWS // 8)
        def _(g):
            for r in range(8):
                at = l * PAD + EDGE + g * 8 + r
                state[pl.ds(at, 4, stride=field), :] = slots[place[l, g * 8 + r]]

    for copy in halos:
        copy.wait()
    for side, at in ((0, EDGE + ROWS), (1, EDGE - HALO)):
        for l in range(LEVELS):
            for r in range(HALO):
                state[pl.ds(l * PAD + at + r, 4, stride=field), :] = halo_in[side, l * HALO + r]

    def start_field(f, l):
        return state[pl.ds(pl.multiple_of(f * field + l * PAD, 8), PAD), :]

    both[...] = jnp.zeros_like(both)

    @pl.loop(0, LEVELS)
    def _(l):
        m = mask[...]
        t, s, u, v = (start_field(f, l) for f in range(4))
        tx, ty, tl = stencil(t)
        sx, sy, sl = stencil(s)
        t1 = t + m * (scale[l] * tl - u * tx - v * ty)
        s1 = s + m * (scale[l] * sl - u * sx - v * sy)
        q = (-0.25 * t + 0.75 * s - 0.05 * t * t) * thick[l]
        layer[l] = q
        both[0] += q
        heat[l] = t1
        grad[0, l] = tx
        grad[1, l] = ty
        grad[2, l] = sx
        grad[3, l] = sy
        a, b = mul_t[l], mul_s[l]
        mu = base_u[l] - a * slope_x(t1) - b * slope_x(s1)
        mv = base_v[l] - a * slope_y(t1) - b * slope_y(s1)
        c, d = m * mu, m * mv
        push_u[l] = mu - 0.5 * d
        push_v[l] = mv + 0.5 * c
        p = slope_x(c) + slope_y(d)
        drive_p[l] = p
        both[1] += p

    to_slabs(lambda turn: both.at[turn], boths, both_send, both_recv)

    def inner(l, running):
        m = mask[...]
        q = layer[l]
        running = running + q
        pressure = 0.2 * (running - 0.5 * q)
        u, v = start_field(2, l), start_field(3, l)
        u1 = u + m * (0.5 * v - slope_x(pressure))
        v1 = v - m * (0.5 * u + slope_y(pressure))
        a, b = mul_t[l], mul_s[l]
        later_t[l] = base_t[l] - bend[l] * heat[l] + slope_x(a * u1) + slope_y(a * v1)
        later_s[l] = base_s[l] + slope_x(b * u1) + slope_y(b * v1)
        return running

    lax.fori_loop(0, LEVELS, inner, jnp.zeros((PAD, CELLS), jnp.float32))

    def upward(j, running):
        l = LEVELS - 1 - j
        p = drive_p[l]
        running = running + p
        adj_q[l] = running - 0.5 * p
        return running

    lax.fori_loop(0, LEVELS, upward, jnp.zeros((PAD, CELLS), jnp.float32))

    whole(boths, both_recv)
    upper = jnp.zeros((PAD, CELLS), jnp.float32)
    lower = jnp.zeros((PAD, CELLS), jnp.float32)
    for k in range(1, SLABS):
        came = boths[k - 1]
        upper += jnp.where(k <= lev, came, 0.0)
        lower += jnp.where(k > lev, came, 0.0)
    m = mask[...]
    total[...] = lower
    totals[0] = 0.2 * m * slope_x(upper)
    totals[1] = 0.2 * m * slope_y(upper)

    @pl.loop(0, LEVELS)
    def _(l):
        m = mask[...]
        gx, gy = totals[0], totals[1]
        a, b = mul_t[l], mul_s[l]
        mt = later_t[l] - slope_x(a * gx) - slope_y(a * gy)
        ms = later_s[l] - slope_x(b * gx) - slope_y(b * gy)
        a, b = m * mt, m * ms
        t, u, v = start_field(0, l), start_field(2, l), start_field(3, l)
        density = 0.2 * (adj_q[l] + total[...]) * thick[l]
        here = slice(EDGE, EDGE + ROWS)
        out_t = mt + scale[l] * laplace(a) + slope_x(a * u) + slope_y(a * v) - density * (0.25 + 0.1 * t)
        out_s = ms + scale[l] * laplace(b) + slope_x(b * u) + slope_y(b * v) + 0.75 * density
        out_u = push_u[l] - a * grad[0, l] - b * grad[2, l]
        out_v = push_v[l] - a * grad[1, l] - b * grad[3, l]
        result[0, l] = out_t[here]
        result[1, l] = out_s[here]
        result[2, l] = out_u[here]
        result[3, l] = out_v[here]

    finish = pltpu.make_async_copy(result, out, out_sem)
    finish.start()
    whole(arrived, slot_send)
    whole(boths, both_send)
    finish.wait()


def per_device(store, placement, wet, kappa, thickness, cotangent):
    padded = pltpu.VMEM((LEVELS, PAD, CELLS), jnp.float32)
    plane = pltpu.VMEM((PAD, CELLS), jnp.float32)
    planes = pltpu.VMEM((SLABS - 1, PAD, CELLS), jnp.float32)
    dma = pltpu.SemaphoreType.DMA
    scratch = [
        pltpu.VMEM((TILES * SLOTS, 4, CELLS), jnp.float32),
        pltpu.VMEM((4 * LEVELS * PAD, CELLS), jnp.float32),
        pltpu.VMEM((2, LEVELS * HALO, 4, CELLS), jnp.float32),
        pltpu.VMEM((2, LEVELS * HALO, 4, CELLS), jnp.float32),
        pltpu.SMEM((LEVELS, ROWS), jnp.int32),
        pltpu.VMEM((ROWS, CELLS), jnp.int32),
        pltpu.SMEM((LEVELS,), jnp.float32),
        pltpu.SMEM((LEVELS,), jnp.float32),
        pltpu.VMEM((4, LEVELS, ROWS, CELLS), jnp.float32),
        pltpu.VMEM((2, 40, CELLS), jnp.float32),
        pltpu.VMEM((2, 40, CELLS), jnp.float32),
        pltpu.VMEM((4, LEVELS, PAD, CELLS), jnp.float32),
        plane,
        plane,
        planes,
        pltpu.VMEM((2, PAD, CELLS), jnp.float32),
        planes,
        padded, padded, padded, padded, padded, padded, padded, padded,
        padded, padded, padded, padded,
        pltpu.VMEM((4, LEVELS, PAD, CELLS), jnp.float32),
        padded, padded, padded,
        pltpu.VMEM((4, LEVELS, ROWS, CELLS), jnp.float32),
        dma((5,)),
        pltpu.SemaphoreType.REGULAR((3,)),
        dma, dma, dma,
        dma((2,)), dma((2,)), dma((2,)), dma((2,)),
        dma, dma, dma, dma, dma,
    ]
    return pl.pallas_call(
        kernel,
        out_shape=jax.ShapeDtypeStruct(cotangent.shape, jnp.float32),
        in_specs=[pl.BlockSpec(memory_space=pl.ANY)] * 6,
        out_specs=pl.BlockSpec(memory_space=pl.ANY),
        scratch_shapes=scratch,
        compiler_params=pltpu.CompilerParams(
            collective_id=0, has_side_effects=True, vmem_limit_bytes=32 << 20
        ),
    )(
        store.reshape(TILES * SLOTS, 4, CELLS), placement, wet, kappa, thickness, cotangent
    )


def solution(mesh):
    placed = (
        P("lev", "tile", None, None, None),
        P("lev", "tile"),
        P("tile", None),
        P("lev"),
        P("lev"),
        P(None, "lev", "tile", None),
    )
    return jax.shard_map(
        per_device,
        mesh=mesh,
        in_specs=placed,
        out_specs=P(None, "lev", "tile", None),
        check_vma=False,
    )
```

time: 198 us -> 81 us (0.41)
  Pallas kernels: 0 us -> 75.5 us
  blocking collectives: 61.2 us -> 0 us
  waiting for transfers between devices: 61.1 us -> 0 us
  starting transfers between devices: 51.3 us -> 0 us
  local copies, waits for them, and re-layouts: 13.8 us -> 5.17 us
  other arithmetic: 7.8 us -> 0 us
    pallas_call x0 -> x1, Pallas kernels: none -> 75.5 us  [per_device(): pl.pallas_call(kernel, out_shape=jax.ShapeDtypeStruct(cotangent.shape, jn...]
    all_gather x4 -> x0, blocking collectives: 61.2 us -> none  [carried_in(): everything = lax.all_gather(x, axis)]
    all_to_all x1 -> x0, waiting for transfers between devices: 50.6 us -> none  [per_device(): lax.all_to_all(held, 'tile', split_axis=0, concat_axis=0, tiled=True)]
    ppermute x8 -> x0, starting transfers between devices: 32 us -> none  [the longest x4 14.1 us: passed_along(): return lax.ppermute(block, axis, route)]
    all_to_all x1 -> x0, starting transfers between devices: 19.3 us -> none  [per_device(): lax.all_to_all(held, 'tile', split_axis=0, concat_axis=0, tiled=True)]
    ppermute x8 -> x0, waiting for transfers between devices: 10.4 us -> none  [the longest x4 9.38 us: passed_along(): return lax.ppermute(block, axis, route)]
    slice x11 -> x0, local copies, waits for them, and re-layouts: 3.6 us -> none  [the longest x6 3.24 us: slope_y(): return (jnp.roll(center, -1, 2) - jnp.roll(center, 1, 2)) * 0.5]
    another operation x7 -> x0, other arithmetic: 2.6 us -> none  [the longest x3 1.2 us: backward(): return jnp.stack([adjoint_warm, adjoint_salt, adjoint_zonal, adjoint_merid])]
  transfers between devices with their start and end apart: 9 -> 0, of which waited for: 5 -> 0; matrix products, arithmetic and copies ran while one was open for 1% -> 0% of each run, Pallas kernels for 0% -> 0%
where the time goes in v1:
time: 81 us; the launch traced here: 80.7 us
  Pallas kernels  75.5 us (93%)
  local copies, waits for them, and re-layouts  5.17 us (6%)
    pallas_call x1, Pallas kernels, per_device(): pl.pallas_call(kernel, out_shape=jax.ShapeDtypeStruct(cotangent.shape, jn...  75.5 us
    unnamed x13, local copies, waits for them, and re-layouts  5.17 us

profile of v1, /device:TPU:1, one launch (start us, length us, event | category | flops | bytes accessed | tf_op | source)
XLA Modules:
  0.0 80.7 jit_solution(4655124506849086412)
XLA Ops:
  0.0 0.0 copy-start.5
  0.0 0.0 copy-start.4
  0.0 0.7 copy-done.5
  0.7 0.0 copy-done.4
  0.7 0.0 copy-start
  0.7 1.2 %copy-done = f32[1,64,8,4,128]{4,3,2,1,0:T(4,128)S(1)} copy-done((f32[1,64,8,4,128]{4,3,2,1,0:T(4,128)S(1)}, f32[1,64,8,4,128]{4,3,2,1,0:T(4,128)}, u32[]{:S(2)}) %copy-start) | copy-done | bytes 1048600
  1.9 0.0 copy-start.1
  1.9 1.0 %copy-done.1 = f32[4,4,64,128]{3,2,1,0:T(8,128)S(1)} copy-done((f32[4,4,64,128]{3,2,1,0:T(8,128)S(1)}, f32[4,4,64,128]{3,2,1,0:T(8,128)}, u32[]{:S(2)}) %copy-start.1) | copy-done | bytes 524312
  2.9 0.0 copy-start.2
  2.9 0.8 copy-done.2
  3.7 0.0 copy-start.3
  3.7 0.7 copy-done.3
  4.4 75.5 %shard_map.64 = f32[4,4,64,128]{3,2,1,0:T(8,128)S(1)} custom-call(f32[512,4,128]{2,1,0:T(4,128)S(1)} %bitcast.1, s32[4,64]{1,0:T(4,128)S(1)} %copy-done.3, s32[64,128]{1,0:T(8,128)S(1)} %copy-done.2, f32[4]{0:T(128)S(1)} %copy-done.4, f32[4]{0:T(128)S(1)} %copy-done.5, f32[4,4,64,128]{3,2,1,0:T(8,128)S(1)} %copy-done.1), custom_call_target="tpu_custom_call" | custom-call | tf_op jit(solution)/shard_map/pallas_call | solution.py:379
  79.9 0.8 copy.8
Async XLA Ops:
  0.0 0.7 copy-start.5
  0.0 0.7 copy-start.4
  0.7 1.2 %copy-start = (f32[1,64,8,4,128]{4,3,2,1,0:T(4,128)S(1)}, f32[1,64,8,4,128]{4,3,2,1,0:T(4,128)}, u32[]{:S(2)}) copy-start(f32[1,64,8,4,128]{4,3,2,1,0:T(4,128)} %param.6) | copy-start | bytes 3145732
  1.9 1.0 %copy-start.1 = (f32[4,4,64,128]{3,2,1,0:T(8,128)S(1)}, f32[4,4,64,128]{3,2,1,0:T(8,128)}, u32[]{:S(2)}) copy-start(f32[4,4,64,128]{3,2,1,0:T(8,128)} %cotangent.1) | copy-start | bytes 1572868
  2.9 0.8 copy-start.2
  3.7 0.7 copy-start.3

commit v2 on v1

--- a/solution.py
+++ b/solution.py
@@ -1,3 +1,5 @@
+import functools
+
 import jax
 import jax.numpy as jnp
 from jax import lax
@@ -17,6 +19,10 @@
 SIDE = 4
 SLABS = 8
 HALO = 3
+EARLY = (0, 1, 2, 3, 4)
+ORDER = (0, 1, 2, 3, 4, 5, 6, 15, 7, 14, 13, 8, 12, 9, 10, 11)
+SPLIT = 5
+NEAR = 4
 RIM = 2
 
 
@@ -25,7 +31,7 @@
 
 
 def after(x):
-    return pltpu.roll(x, PAD - 1, 0)
+    return pltpu.roll(x, x.shape[0] - 1, 0)
 
 
 def slope_x(x):
@@ -49,11 +55,11 @@
 def kernel(
     store, placement, wet, kappa, thickness, cotangent, out,
     slots, state, halo_out, halo_in, place, wet_in, scale, thick, cot, rim_out, rim_in,
-    lam, mask, total, totals, both, boths,
+    lam, mask, total, totals, both, mid, mids, edge, edges,
     drive_p, mul_t, mul_s, base_t, base_s, base_u, base_v, bend,
     heat, layer, push_u, push_v, grad, later_t, later_s, adj_q, result,
     load_sem, ready_sem, slot_send, slot_recv, own_sem, halo_send, halo_recv,
-    rim_send, rim_recv, total_send, total_recv, both_send, both_recv, out_sem,
+    rim_send, rim_recv, total_send, total_recv, mid_send, mid_recv, edge_send, edge_recv, out_sem,
 ):
     me = lax.axis_index("tile")
     lev = lax.axis_index("lev")
@@ -82,6 +88,10 @@
     ]
     for load in loads:
         load.start()
+
+    def is_early(plane):
+        return functools.reduce(lambda found, e: found | (plane == e), EARLY, plane < 0)
+
     own = pltpu.make_async_copy(
         store.at[pl.ds(me * SLOTS, SLOTS)], slots.at[pl.ds(me * SLOTS, SLOTS)], own_sem
     )
@@ -97,12 +107,43 @@
             device_id_type=MESH,
         ).start()
 
-    def send_ring(first, last):
-        @pl.loop(first * 8, last * 8)
-        def _(i):
-            reach = i // 8
-            towards = 1 - 2 * lax.rem(i, 2)
-            send_slots(tile_at(reach * towards, lax.rem(i // 2, SIDE)))
+    def send_near(reach):
+        for dz in (reach, -reach):
+            to_z = lax.rem(z + (dz + RING), RING)
+
+            @pl.when(is_early(to_z) if reach > 2 else z >= 0)
+            def _():
+                @pl.loop(0, SIDE)
+                def _(dy):
+                    send_slots(tile_at(dz, dy))
+
+    def send_planes(planes):
+        for to_z in planes:
+            gap = lax.rem(z + (RING - to_z), RING)
+            gap = jnp.minimum(gap, RING - gap)
+
+            @pl.when(gap > (NEAR if to_z in EARLY else 2))
+            def _():
+                @pl.loop(0, SIDE)
+                def _(dy):
+                    if to_z == RING - 1:
+
+                        @pl.when(dy > 0)
+                        def _():
+                            send_slots(to_z * SIDE + dy - 1)
+                    else:
+                        send_slots(to_z * SIDE + lax.rem(y + dy, SIDE))
+
+    pl.semaphore_wait(greet, 7 + SLABS - 1)
+    for dy in (1, 2, 3):
+        signal(ready_sem.at[0], tile=tile_at(0, dy))
+    for dy in (1, 2, 3):
+        send_slots(tile_at(0, dy))
+    pl.semaphore_wait(ready_sem.at[0], 3)
+    for dz in (2, -2):
+        signal(ready_sem.at[1], tile=tile_at(dz, 0))
+    send_near(1)
+    send_near(2)
 
     for load in loads:
         load.wait()
@@ -115,15 +156,6 @@
             lam[f, l, EDGE : EDGE + ROWS] = cot[f, l]
             rim_out[0, i * RIM : (i + 1) * RIM] = cot[f, l, 0:RIM]
             rim_out[1, i * RIM : (i + 1) * RIM] = cot[f, l, ROWS - RIM : ROWS]
-
-    pl.semaphore_wait(greet, 7 + SLABS - 1)
-    for dy in (1, 2, 3):
-        signal(ready_sem.at[0], tile=tile_at(0, dy))
-    for dy in (1, 2, 3):
-        send_slots(tile_at(0, dy))
-    pl.semaphore_wait(ready_sem.at[0], 3)
-    for dz in (2, -2):
-        signal(ready_sem.at[1], tile=tile_at(dz, 0))
 
     left, right = lax.rem(me + TILES - 1, TILES), lax.rem(me + 1, TILES)
 
@@ -143,12 +175,18 @@
     rims = to_neighbours(rim_out, rim_in, rim_send, rim_recv)
     for copy in rims:
         copy.start()
-    send_ring(1, 3)
+
     pl.semaphore_wait(ready_sem.at[1], 2)
     for dz in (4, -4):
         signal(ready_sem.at[2], tile=tile_at(dz, 0))
-    send_ring(3, 5)
+    send_near(3)
+    send_near(4)
     pl.semaphore_wait(ready_sem.at[2], 2)
+    @pl.when((z < RING - 1 - 2) & (z > 1))
+    def _():
+        send_slots(TILES - 1)
+
+    send_planes(ORDER[:SPLIT])
 
     for copy in rims:
         copy.wait()
@@ -185,13 +223,7 @@
 
     to_slabs(lambda turn: total, totals, total_send, total_recv)
 
-    for dy in range(SIDE):
-        send_slots(tile_at(RING // 2, dy))
-
-    @pl.loop(0, 24)
-    def _(i):
-        towards = 1 - 2 * lax.rem(i, 2)
-        send_slots(tile_at((7 - i // 8) * towards, lax.rem(i // 2, SIDE)))
+    send_planes(ORDER[SPLIT:])
 
     whole(totals, total_recv)
     whole(totals, total_send)
@@ -239,6 +271,40 @@
                 at = l * PAD + EDGE + g * 8 + r
                 state[pl.ds(at, 4, stride=field), :] = slots[place[l, g * 8 + r]]
 
+    def start_field(f, l):
+        return state[pl.ds(pl.multiple_of(f * field + l * PAD, 8), PAD), :]
+
+    def first_step(l, cut):
+        m = cut(mask[...])
+        t, s, u, v = (cut(start_field(f, l)) for f in range(4))
+        tx, ty, tl = stencil(t)
+        sx, sy, sl = stencil(s)
+        t1 = t + m * (scale[l] * tl - u * tx - v * ty)
+        s1 = s + m * (scale[l] * sl - u * sx - v * sy)
+        q = (-0.25 * t + 0.75 * s - 0.05 * t * t) * thick[l]
+        a, b = cut(mul_t[l]), cut(mul_s[l])
+        mu = cut(base_u[l]) - a * slope_x(t1) - b * slope_x(s1)
+        mv = cut(base_v[l]) - a * slope_y(t1) - b * slope_y(s1)
+        c, d = m * mu, m * mv
+        p = slope_x(c) + slope_y(d)
+        return q, t1, tx, ty, sx, sy, mu - 0.5 * d, mv + 0.5 * c, p
+
+    kept = (
+        layer, heat, grad.at[0], grad.at[1], grad.at[2], grad.at[3], push_u, push_v, drive_p,
+    )
+
+    mid[...] = jnp.zeros_like(mid)
+
+    @pl.loop(0, LEVELS)
+    def _(l):
+        values = first_step(l, lambda x: x)
+        for ref, value in zip(kept, values):
+            ref[l] = value
+        mid[0] += values[0][8 : PAD - 8]
+        mid[1] += values[-1][8 : PAD - 8]
+
+    to_slabs(lambda turn: mid.at[turn], mids, mid_send, mid_recv)
+
     for copy in halos:
         copy.wait()
     for side, at in ((0, EDGE + ROWS), (1, EDGE - HALO)):
@@ -246,38 +312,19 @@
             for r in range(HALO):
                 state[pl.ds(l * PAD + at + r, 4, stride=field), :] = halo_in[side, l * HALO + r]
 
-    def start_field(f, l):
-        return state[pl.ds(pl.multiple_of(f * field + l * PAD, 8), PAD), :]
-
-    both[...] = jnp.zeros_like(both)
+    edge[...] = jnp.zeros_like(edge)
 
     @pl.loop(0, LEVELS)
     def _(l):
-        m = mask[...]
-        t, s, u, v = (start_field(f, l) for f in range(4))
-        tx, ty, tl = stencil(t)
-        sx, sy, sl = stencil(s)
-        t1 = t + m * (scale[l] * tl - u * tx - v * ty)
-        s1 = s + m * (scale[l] * sl - u * sx - v * sy)
-        q = (-0.25 * t + 0.75 * s - 0.05 * t * t) * thick[l]
-        layer[l] = q
-        both[0] += q
-        heat[l] = t1
-        grad[0, l] = tx
-        grad[1, l] = ty
-        grad[2, l] = sx
-        grad[3, l] = sy
-        a, b = mul_t[l], mul_s[l]
-        mu = base_u[l] - a * slope_x(t1) - b * slope_x(s1)
-        mv = base_v[l] - a * slope_y(t1) - b * slope_y(s1)
-        c, d = m * mu, m * mv
-        push_u[l] = mu - 0.5 * d
-        push_v[l] = mv + 0.5 * c
-        p = slope_x(c) + slope_y(d)
-        drive_p[l] = p
-        both[1] += p
-
-    to_slabs(lambda turn: both.at[turn], boths, both_send, both_recv)
+        values = first_step(l, lambda x: jnp.concatenate([x[:16], x[PAD - 16 :]], 0))
+        for ref, value in zip(kept, values):
+            ref[l, :8] = value[:8]
+            ref[l, PAD - 8 :] = value[24:]
+        for side, value in ((0, values[0]), (1, values[-1])):
+            edge[side, :8] += value[:8]
+            edge[side, 8:] += value[24:]
+
+    to_slabs(lambda turn: edge.at[turn], edges, edge_send, edge_recv)
 
     def inner(l, running):
         m = mask[...]
@@ -303,15 +350,22 @@
 
     lax.fori_loop(0, LEVELS, upward, jnp.zeros((PAD, CELLS), jnp.float32))
 
-    whole(boths, both_recv)
-    upper = jnp.zeros((PAD, CELLS), jnp.float32)
-    lower = jnp.zeros((PAD, CELLS), jnp.float32)
-    for k in range(1, SLABS):
-        came = boths[k - 1]
-        upper += jnp.where(k <= lev, came, 0.0)
-        lower += jnp.where(k > lev, came, 0.0)
-    m = mask[...]
-    total[...] = lower
+    def gather_totals(came):
+        upper = jnp.zeros(came.shape[1:], jnp.float32)
+        lower = jnp.zeros(came.shape[1:], jnp.float32)
+        for k in range(1, SLABS):
+            upper += jnp.where(k <= lev, came[k - 1], 0.0)
+            lower += jnp.where(k > lev, came[k - 1], 0.0)
+        return upper, lower
+
+    whole(mids, mid_recv)
+    for i, value in enumerate(gather_totals(mids)):
+        both[i, 8 : PAD - 8] = value
+    whole(edges, edge_recv)
+    for i, value in enumerate(gather_totals(edges)):
+        both[i, :8] = value[:8]
+        both[i, PAD - 8 :] = value[8:]
+    m, upper = mask[...], both[0]
     totals[0] = 0.2 * m * slope_x(upper)
     totals[1] = 0.2 * m * slope_y(upper)
 
@@ -324,7 +378,7 @@
         ms = later_s[l] - slope_x(b * gx) - slope_y(b * gy)
         a, b = m * mt, m * ms
         t, u, v = start_field(0, l), start_field(2, l), start_field(3, l)
-        density = 0.2 * (adj_q[l] + total[...]) * thick[l]
+        density = 0.2 * (adj_q[l] + both[1]) * thick[l]
         here = slice(EDGE, EDGE + ROWS)
         out_t = mt + scale[l] * laplace(a) + slope_x(a * u) + slope_y(a * v) - density * (0.25 + 0.1 * t)
         out_s = ms + scale[l] * laplace(b) + slope_x(b * u) + slope_y(b * v) + 0.75 * density
@@ -334,12 +388,13 @@
         result[1, l] = out_s[here]
         result[2, l] = out_u[here]
         result[3, l] = out_v[here]
-
-    finish = pltpu.make_async_copy(result, out, out_sem)
-    finish.start()
+        pltpu.make_async_copy(result.at[:, l], out.at[:, l], out_sem.at[l]).start()
+
     whole(arrived, slot_send)
-    whole(boths, both_send)
-    finish.wait()
+    whole(mids, mid_send)
+    whole(edges, edge_send)
+    for l in range(LEVELS):
+        pltpu.make_async_copy(result.at[:, l], out.at[:, l], out_sem.at[l]).wait()
 
 
 def per_device(store, placement, wet, kappa, thickness, cotangent):
@@ -364,7 +419,10 @@
         plane,
         planes,
         pltpu.VMEM((2, PAD, CELLS), jnp.float32),
-        planes,
+        pltpu.VMEM((2, PAD - 16, CELLS), jnp.float32),
+        pltpu.VMEM((SLABS - 1, PAD - 16, CELLS), jnp.float32),
+        pltpu.VMEM((2, 16, CELLS), jnp.float32),
+        pltpu.VMEM((SLABS - 1, 16, CELLS), jnp.float32),
         padded, padded, padded, padded, padded, padded, padded, padded,
         padded, padded, padded, padded,
         pltpu.VMEM((4, LEVELS, PAD, CELLS), jnp.float32),
@@ -374,16 +432,17 @@
         pltpu.SemaphoreType.REGULAR((3,)),
         dma, dma, dma,
         dma((2,)), dma((2,)), dma((2,)), dma((2,)),
-        dma, dma, dma, dma, dma,
+        dma, dma, dma, dma, dma, dma,
+        dma((LEVELS,)),
     ]
     return pl.pallas_call(
         kernel,
         out_shape=jax.ShapeDtypeStruct(cotangent.shape, jnp.float32),
-        in_specs=[pl.BlockSpec(memory_space=pl.ANY)] * 6,
-        out_specs=pl.BlockSpec(memory_space=pl.ANY),
+        in_specs=[pl.BlockSpec(memory_space=pltpu.HBM)] * 6,
+        out_specs=pl.BlockSpec(memory_space=pltpu.HBM),
         scratch_shapes=scratch,
         compiler_params=pltpu.CompilerParams(
-            collective_id=0, has_side_effects=True, vmem_limit_bytes=32 << 20
+            collective_id=0, has_side_effects=True, vmem_limit_bytes=60 << 20
         ),
     )(
         store.reshape(TILES * SLOTS, 4, CELLS), placement, wet, kappa, thickness, cotangent

time: 81 us -> 75.8 us (0.936)
  local copies, waits for them, and re-layouts: 5.17 us -> 1.89 us
  Pallas kernels: 75.5 us -> 72.8 us
    unnamed x13 -> x1, local copies, waits for them, and re-layouts: 5.17 us -> 1.89 us
    pallas_call x1, Pallas kernels: 75.5 us -> 72.8 us  [per_device(): pl.pallas_call(kernel, out_shape=jax.ShapeDtypeStruct(cotangent.shape, jn...]
where the time goes in v2:
time: 75.8 us; the launch traced here: 74.7 us
  Pallas kernels  72.8 us (96%)
  local copies, waits for them, and re-layouts  1.89 us (2%)
    pallas_call x1, Pallas kernels, per_device(): pl.pallas_call(kernel, out_shape=jax.ShapeDtypeStruct(cotangent.shape, jn...  72.8 us
    unnamed x1, local copies, waits for them, and re-layouts  1.89 us

profile of v2, /device:TPU:1, one launch (start us, length us, event | category | flops | bytes accessed | tf_op | source)
XLA Modules:
  0.0 74.7 jit_solution(13266354368812262804)
XLA Ops:
  0.0 72.8 %shard_map.64 = f32[4,4,64,128]{3,2,1,0:T(8,128)} custom-call(f32[512,4,128]{2,1,0:T(4,128)} %bitcast.1, s32[4,64]{1,0:T(4,128)} %placement.1, s32[64,128]{1,0:T(8,128)} %wet.1, f32[4]{0:T(128)} %kappa.1, f32[4]{0:T(128)} %thickness.1, f32[4,4,64,128]{3,2,1,0:T(8,128)} %cotangent.1), custom_call_target="tpu_custom_call" | custom-call | tf_op jit(solution)/shard_map/pallas_call | solution.py:438
  72.8 1.9 %copy.8 = f32[4,4,64,128]{3,2,1,0:T(8,128)} copy(f32[4,4,64,128]{3,2,1,0:T(8,128)} %shard_map.64) | data formatting | bytes 1048576

commit v3 on v2

--- a/solution.py
+++ b/solution.py
@@ -19,10 +19,11 @@
 SIDE = 4
 SLABS = 8
 HALO = 3
-EARLY = (0, 1, 2, 3, 4)
+EARLY = (0, 1, 2, 3)
 ORDER = (0, 1, 2, 3, 4, 5, 6, 15, 7, 14, 13, 8, 12, 9, 10, 11)
 SPLIT = 5
 NEAR = 4
+UNROLL = True
 RIM = 2
 
 
@@ -57,9 +58,9 @@
     slots, state, halo_out, halo_in, place, wet_in, scale, thick, cot, rim_out, rim_in,
     lam, mask, total, totals, both, mid, mids, edge, edges,
     drive_p, mul_t, mul_s, base_t, base_s, base_u, base_v, bend,
-    heat, layer, push_u, push_v, grad, later_t, later_s, adj_q, result,
+    heat, layer, push_u, push_v, grad, later_t, later_s, adj_q, moved,
     load_sem, ready_sem, slot_send, slot_recv, own_sem, halo_send, halo_recv,
-    rim_send, rim_recv, total_send, total_recv, mid_send, mid_recv, edge_send, edge_recv, out_sem,
+    rim_send, rim_recv, total_send, total_recv, mid_send, mid_recv, edge_send, edge_recv,
 ):
     me = lax.axis_index("tile")
     lev = lax.axis_index("lev")
@@ -189,7 +190,7 @@
     send_planes(ORDER[:SPLIT])
 
     for copy in rims:
-        copy.wait()
+        copy.wait_recv()
     for side, at in ((0, EDGE + ROWS), (1, EDGE - RIM)):
         mask[at : at + RIM] = rim_in[side, 32:34]
         for f in range(4):
@@ -241,6 +242,12 @@
         a, b = m * lt, m * ls
         mul_t[l] = a
         mul_s[l] = b
+        for i, x in enumerate((a, b)):
+            x = 0.5 * x
+            moved[i, l] = after(x)
+            moved[i + 2, l] = before(x)
+            moved[i + 4, l] = pltpu.roll(x, CELLS - 1, 1)
+            moved[i + 6, l] = pltpu.roll(x, 1, 1)
         base_t[l] = lt + scale[l] * laplace(a) - 0.25 * density
         base_s[l] = ls + scale[l] * laplace(b) + 0.75 * density
         base_u[l] = lu - 0.5 * (m * lv)
@@ -306,25 +313,24 @@
     to_slabs(lambda turn: mid.at[turn], mids, mid_send, mid_recv)
 
     for copy in halos:
-        copy.wait()
+        copy.wait_recv()
     for side, at in ((0, EDGE + ROWS), (1, EDGE - HALO)):
         for l in range(LEVELS):
             for r in range(HALO):
                 state[pl.ds(l * PAD + at + r, 4, stride=field), :] = halo_in[side, l * HALO + r]
 
-    edge[...] = jnp.zeros_like(edge)
-
-    @pl.loop(0, LEVELS)
-    def _(l):
-        values = first_step(l, lambda x: jnp.concatenate([x[:16], x[PAD - 16 :]], 0))
-        for ref, value in zip(kept, values):
+    found = [
+        first_step(l, lambda x: jnp.concatenate([x[:16], x[PAD - 16 :]], 0)) for l in range(LEVELS)
+    ]
+    for side, sums in ((0, sum(v[0] for v in found)), (1, sum(v[-1] for v in found))):
+        edge[side, :8] = sums[:8]
+        edge[side, 8:] = sums[24:]
+
+    to_slabs(lambda turn: edge.at[turn], edges, edge_send, edge_recv)
+    for l in range(LEVELS):
+        for ref, value in zip(kept, found[l]):
             ref[l, :8] = value[:8]
             ref[l, PAD - 8 :] = value[24:]
-        for side, value in ((0, values[0]), (1, values[-1])):
-            edge[side, :8] += value[:8]
-            edge[side, 8:] += value[24:]
-
-    to_slabs(lambda turn: edge.at[turn], edges, edge_send, edge_recv)
 
     def inner(l, running):
         m = mask[...]
@@ -366,35 +372,47 @@
         both[i, :8] = value[:8]
         both[i, PAD - 8 :] = value[8:]
     m, upper = mask[...], both[0]
-    totals[0] = 0.2 * m * slope_x(upper)
-    totals[1] = 0.2 * m * slope_y(upper)
-
-    @pl.loop(0, LEVELS)
+    gx, gy = 0.2 * m * slope_x(upper), 0.2 * m * slope_y(upper)
+    totals[0] = after(gx)
+    totals[1] = before(gx)
+    totals[2] = pltpu.roll(gy, CELLS - 1, 1)
+    totals[3] = pltpu.roll(gy, 1, 1)
+
+    def spread(x, u, v, k):
+        near, along, across = k * x, 0.5 * (x * u), 0.5 * (x * v)
+        rows = after(near + along) + before(near - along)
+        cells = pltpu.roll(near + across, CELLS - 1, 1) + pltpu.roll(near - across, 1, 1)
+        return rows + cells - 4.0 * near
+
+    @pl.loop(0, LEVELS, unroll=UNROLL)
     def _(l):
         m = mask[...]
-        gx, gy = totals[0], totals[1]
-        a, b = mul_t[l], mul_s[l]
-        mt = later_t[l] - slope_x(a * gx) - slope_y(a * gy)
-        ms = later_s[l] - slope_x(b * gx) - slope_y(b * gy)
+
+        def carried(i):
+            down, up = moved[i, l] * totals[0], moved[i + 2, l] * totals[1]
+            right, left = moved[i + 4, l] * totals[2], moved[i + 6, l] * totals[3]
+            return (down - up) + (right - left)
+
+        mt = later_t[l] - carried(0)
+        ms = later_s[l] - carried(1)
         a, b = m * mt, m * ms
         t, u, v = start_field(0, l), start_field(2, l), start_field(3, l)
         density = 0.2 * (adj_q[l] + both[1]) * thick[l]
         here = slice(EDGE, EDGE + ROWS)
-        out_t = mt + scale[l] * laplace(a) + slope_x(a * u) + slope_y(a * v) - density * (0.25 + 0.1 * t)
-        out_s = ms + scale[l] * laplace(b) + slope_x(b * u) + slope_y(b * v) + 0.75 * density
+        out_t = mt + spread(a, u, v, scale[l]) - density * (0.25 + 0.1 * t)
+        out_s = ms + spread(b, u, v, scale[l]) + 0.75 * density
         out_u = push_u[l] - a * grad[0, l] - b * grad[2, l]
         out_v = push_v[l] - a * grad[1, l] - b * grad[3, l]
-        result[0, l] = out_t[here]
-        result[1, l] = out_s[here]
-        result[2, l] = out_u[here]
-        result[3, l] = out_v[here]
-        pltpu.make_async_copy(result.at[:, l], out.at[:, l], out_sem.at[l]).start()
-
+        out[0, l] = out_t[here]
+        out[1, l] = out_s[here]
+        out[2, l] = out_u[here]
+        out[3, l] = out_v[here]
+
+    for copy in rims + halos:
+        copy.wait_send()
     whole(arrived, slot_send)
     whole(mids, mid_send)
     whole(edges, edge_send)
-    for l in range(LEVELS):
-        pltpu.make_async_copy(result.at[:, l], out.at[:, l], out_sem.at[l]).wait()
 
 
 def per_device(store, placement, wet, kappa, thickness, cotangent):
@@ -427,25 +445,29 @@
         padded, padded, padded, padded,
         pltpu.VMEM((4, LEVELS, PAD, CELLS), jnp.float32),
         padded, padded, padded,
-        pltpu.VMEM((4, LEVELS, ROWS, CELLS), jnp.float32),
+        pltpu.VMEM((8, LEVELS, PAD, CELLS), jnp.float32),
         dma((5,)),
         pltpu.SemaphoreType.REGULAR((3,)),
         dma, dma, dma,
         dma((2,)), dma((2,)), dma((2,)), dma((2,)),
         dma, dma, dma, dma, dma, dma,
-        dma((LEVELS,)),
     ]
     return pl.pallas_call(
         kernel,
         out_shape=jax.ShapeDtypeStruct(cotangent.shape, jnp.float32),
         in_specs=[pl.BlockSpec(memory_space=pltpu.HBM)] * 6,
-        out_specs=pl.BlockSpec(memory_space=pltpu.HBM),
+        out_specs=pl.BlockSpec(memory_space=pltpu.VMEM),
         scratch_shapes=scratch,
         compiler_params=pltpu.CompilerParams(
-            collective_id=0, has_side_effects=True, vmem_limit_bytes=60 << 20
+            collective_id=0, has_side_effects=True, vmem_limit_bytes=32 << 20
         ),
     )(
-        store.reshape(TILES * SLOTS, 4, CELLS), placement, wet, kappa, thickness, cotangent
+        *[
+            pltpu.with_memory_space_constraint(x, pltpu.HBM)
+            for x in (
+                store.reshape(TILES * SLOTS, 4, CELLS), placement, wet, kappa, thickness, cotangent,
+            )
+        ]
     )
 
 

time: 75.8 us -> 72.4 us (0.955); the launches traced: 74.7 us -> 72.3 us
  Pallas kernels: 72.8 us -> 71.5 us
  local copies, waits for them, and re-layouts: 1.89 us -> 0.8 us
    pallas_call x1, Pallas kernels: 72.8 us -> 71.5 us  [per_device(): pl.pallas_call(kernel, out_shape=jax.ShapeDtypeStruct(cotangent.shape, jn...]
    unnamed x1, local copies, waits for them, and re-layouts: 1.89 us -> 0.8 us
where the time goes in v3:
time: 72.4 us; the launch traced here: 72.3 us
  Pallas kernels  71.5 us (99%)
  local copies, waits for them, and re-layouts  0.8 us (1%)
    pallas_call x1, Pallas kernels, per_device(): pl.pallas_call(kernel, out_shape=jax.ShapeDtypeStruct(cotangent.shape, jn...  71.5 us

profile of v3, /device:TPU:1, one launch (start us, length us, event | category | flops | bytes accessed | tf_op | source)
XLA Modules:
  0.0 72.3 jit_solution(12106507678720163379)
XLA Ops:
  0.0 71.5 %shard_map.64 = f32[4,4,64,128]{3,2,1,0:T(8,128)S(1)} custom-call(f32[512,4,128]{2,1,0:T(4,128)} %bitcast.1, s32[4,64]{1,0:T(4,128)} %placement.1, s32[64,128]{1,0:T(8,128)} %wet.1, f32[4]{0:T(128)} %kappa.1, f32[4]{0:T(128)} %thickness.1, f32[4,4,64,128]{3,2,1,0:T(8,128)} %cotangent.1), custom_call_target="tpu_custom_call" | custom-call | tf_op jit(solution)/shard_map/pallas_call | solution.py:455
  71.5 0.8 %copy.8 = f32[4,4,64,128]{3,2,1,0:T(8,128)} copy(f32[4,4,64,128]{3,2,1,0:T(8,128)S(1)} %shard_map.64) | data formatting | bytes 1048576

commit v4 on v3

--- a/solution.py
+++ b/solution.py
@@ -19,7 +19,7 @@
 SIDE = 4
 SLABS = 8
 HALO = 3
-EARLY = (0, 1, 2, 3)
+EARLY = (0, 1)
 ORDER = (0, 1, 2, 3, 4, 5, 6, 15, 7, 14, 13, 8, 12, 9, 10, 11)
 SPLIT = 5
 NEAR = 4
@@ -208,7 +208,7 @@
         total[...] += p
 
     def to_slabs(source, incoming, send, recv):
-        for k in range(1, SLABS):
+        for k in (4, 3, 5, 2, 6, 1, 7):
             to = lax.rem(lev + k, SLABS)
             pltpu.make_async_remote_copy(
                 src_ref=source((lev + k) // SLABS),
@@ -262,13 +262,12 @@
     whole(arrived, slot_recv)
 
     field = LEVELS * PAD
-    for l in range(LEVELS):
-        for r in range(HALO):
-            halo_out[0, l * HALO + r] = slots[place[l, r]]
-            halo_out[1, l * HALO + r] = slots[place[l, ROWS - HALO + r]]
     halos = to_neighbours(halo_out, halo_in, halo_send, halo_recv)
-    for copy in halos:
-        copy.start()
+    for side, first in ((1, ROWS - HALO), (0, 0)):
+        for l in range(LEVELS):
+            for r in range(HALO):
+                halo_out[side, l * HALO + r] = slots[place[l, first + r]]
+        halos[side].start()
 
     for l in range(LEVELS):
 

time: 72.4 us -> 71.3 us (0.985)
  the two profiles are of different devices: /device:TPU:1 before, /device:TPU:65 now
where the time goes in v4:
time: 71.3 us; the launch traced here: 71.2 us
  Pallas kernels  70.4 us (99%)
  local copies, waits for them, and re-layouts  0.8 us (1%)
    pallas_call x1, Pallas kernels, per_device(): pl.pallas_call(kernel, out_shape=jax.ShapeDtypeStruct(cotangent.shape, jn...  70.4 us

profile of v4, /device:TPU:65, one launch (start us, length us, event | category | flops | bytes accessed | tf_op | source)
XLA Modules:
  0.0 71.2 jit_solution(2337574064195691865)
XLA Ops:
  0.0 70.4 %shard_map.64 = f32[4,4,64,128]{3,2,1,0:T(8,128)S(1)} custom-call(f32[512,4,128]{2,1,0:T(4,128)} %bitcast.1, s32[4,64]{1,0:T(4,128)} %placement.1, s32[64,128]{1,0:T(8,128)} %wet.1, f32[4]{0:T(128)} %kappa.1, f32[4]{0:T(128)} %thickness.1, f32[4,4,64,128]{3,2,1,0:T(8,128)} %cotangent.1), custom_call_target="tpu_custom_call" | custom-call | tf_op jit(solution)/shard_map/pallas_call | solution.py:454
  70.4 0.8 %copy.8 = f32[4,4,64,128]{3,2,1,0:T(8,128)} copy(f32[4,4,64,128]{3,2,1,0:T(8,128)S(1)} %shard_map.64) | data formatting | bytes 1048576

commit v5 on v4

--- a/solution.py
+++ b/solution.py
@@ -77,8 +77,12 @@
         signal(greet, tile=tile_at(dz, 0))
     for dy in (1, 2, 3):
         signal(greet, tile=tile_at(0, dy))
-    for k in range(1, SLABS):
-        signal(greet, lev=lax.rem(lev + k, SLABS))
+    def nearest_slabs(sem):
+        signal(sem, lev=lev + 1 - 2 * lax.rem(lev, 2))
+        for k in (2, 4, 6):
+            signal(sem, lev=lax.rem(lev + k, SLABS))
+
+    nearest_slabs(greet)
 
     loads = [
         pltpu.make_async_copy(cotangent, cot, load_sem.at[0]),
@@ -114,7 +118,7 @@
 
             @pl.when(is_early(to_z) if reach > 2 else z >= 0)
             def _():
-                @pl.loop(0, SIDE)
+                @pl.loop(0 if reach > 2 else 1, SIDE)
                 def _(dy):
                     send_slots(tile_at(dz, dy))
 
@@ -135,11 +139,14 @@
                     else:
                         send_slots(to_z * SIDE + lax.rem(y + dy, SIDE))
 
-    pl.semaphore_wait(greet, 7 + SLABS - 1)
+    pl.semaphore_wait(greet, 7 + 4)
     for dy in (1, 2, 3):
         signal(ready_sem.at[0], tile=tile_at(0, dy))
+    for dz in (1, -1, 2, -2):
+        send_slots(tile_at(dz, 0))
     for dy in (1, 2, 3):
         send_slots(tile_at(0, dy))
+    nearest_slabs(ready_sem.at[3])
     pl.semaphore_wait(ready_sem.at[0], 3)
     for dz in (2, -2):
         signal(ready_sem.at[1], tile=tile_at(dz, 0))
@@ -222,6 +229,7 @@
     def whole(ref, sem):
         pltpu.make_async_copy(ref, ref, sem).wait()
 
+    pl.semaphore_wait(ready_sem.at[3], 4)
     to_slabs(lambda turn: total, totals, total_send, total_recv)
 
     send_planes(ORDER[SPLIT:])
@@ -446,7 +454,7 @@
         padded, padded, padded,
         pltpu.VMEM((8, LEVELS, PAD, CELLS), jnp.float32),
         dma((5,)),
-        pltpu.SemaphoreType.REGULAR((3,)),
+        pltpu.SemaphoreType.REGULAR((4,)),
         dma, dma, dma,
         dma((2,)), dma((2,)), dma((2,)), dma((2,)),
         dma, dma, dma, dma, dma, dma,

time: 71.3 us -> 70.7 us (level)
  the two profiles are of different devices: /device:TPU:65 before, /device:TPU:97 now
where the time goes in v5:
time: 70.7 us; the launch traced here: 70.6 us
  Pallas kernels  69.8 us (99%)
  local copies, waits for them, and re-layouts  0.8 us (1%)
    pallas_call x1, Pallas kernels, per_device(): pl.pallas_call(kernel, out_shape=jax.ShapeDtypeStruct(cotangent.shape, jn...  69.8 us

profile of v5, /device:TPU:97, one launch (start us, length us, event | category | flops | bytes accessed | tf_op | source)
XLA Modules:
  0.0 70.6 jit_solution(12245914528079556880)
XLA Ops:
  0.0 69.8 %shard_map.64 = f32[4,4,64,128]{3,2,1,0:T(8,128)S(1)} custom-call(f32[512,4,128]{2,1,0:T(4,128)} %bitcast.1, s32[4,64]{1,0:T(4,128)} %placement.1, s32[64,128]{1,0:T(8,128)} %wet.1, f32[4]{0:T(128)} %kappa.1, f32[4]{0:T(128)} %thickness.1, f32[4,4,64,128]{3,2,1,0:T(8,128)} %cotangent.1), custom_call_target="tpu_custom_call" | custom-call | tf_op jit(solution)/shard_map/pallas_call | solution.py:462
  69.8 0.8 %copy.8 = f32[4,4,64,128]{3,2,1,0:T(8,128)} copy(f32[4,4,64,128]{3,2,1,0:T(8,128)S(1)} %shard_map.64) | data formatting | bytes 1048576

commit v6 on v5

--- a/solution.py
+++ b/solution.py
@@ -153,6 +153,9 @@
     send_near(1)
     send_near(2)
 
+    pl.semaphore_wait(ready_sem.at[1], 2)
+    for dz in (4, -4):
+        signal(ready_sem.at[2], tile=tile_at(dz, 0))
     for load in loads:
         load.wait()
     mask[EDGE : EDGE + ROWS] = 0.2 * wet_in[...].astype(jnp.float32)
@@ -184,9 +187,6 @@
     for copy in rims:
         copy.start()
 
-    pl.semaphore_wait(ready_sem.at[1], 2)
-    for dz in (4, -4):
-        signal(ready_sem.at[2], tile=tile_at(dz, 0))
     send_near(3)
     send_near(4)
     pl.semaphore_wait(ready_sem.at[2], 2)

time: 70.7 us -> 70.9 us (level)
  no operation moved by 1% of the time
where the time goes in v6:
time: 70.9 us; the launch traced here: 70.8 us
  Pallas kernels  70 us (99%)
  local copies, waits for them, and re-layouts  0.8 us (1%)
    pallas_call x1, Pallas kernels, per_device(): pl.pallas_call(kernel, out_shape=jax.ShapeDtypeStruct(cotangent.shape, jn...  70 us

profile of v6, /device:TPU:97, one launch (start us, length us, event | category | flops | bytes accessed | tf_op | source)
XLA Modules:
  0.0 70.8 jit_solution(15483339955759662403)
XLA Ops:
  0.0 70.0 %shard_map.64 = f32[4,4,64,128]{3,2,1,0:T(8,128)S(1)} custom-call(f32[512,4,128]{2,1,0:T(4,128)} %bitcast.1, s32[4,64]{1,0:T(4,128)} %placement.1, s32[64,128]{1,0:T(8,128)} %wet.1, f32[4]{0:T(128)} %kappa.1, f32[4]{0:T(128)} %thickness.1, f32[4,4,64,128]{3,2,1,0:T(8,128)} %cotangent.1), custom_call_target="tpu_custom_call" | custom-call | tf_op jit(solution)/shard_map/pallas_call | solution.py:462
  70.0 0.8 %copy.8 = f32[4,4,64,128]{3,2,1,0:T(8,128)} copy(f32[4,4,64,128]{3,2,1,0:T(8,128)S(1)} %shard_map.64) | data formatting | bytes 1048576
